TPU v7x, 128 devices: a whole 4x4x4 slice. The times are simulated.
128 devices in a mesh: cell: 32 (over x, z, y_hi), spec: 4 (over y_lo, core).
Axes of the slice: x: 4, y: 4 (y_hi: 2, y_lo: 2; y = y_hi * 2 + y_lo), z: 4, core: 2. Of those that a mesh axis runs over, the one named last changes fastest.
Arguments:
- fields: bfloat16 [4, 1024, 384], P('spec', 'cell'), may hold values from -6 to 6
- tensors: bfloat16 [16, 384, 384, 384], P('spec', 'cell'), may hold values from -0.0078125 to 0.0078125
- pair_table: int32 [4, 4], replicated, may hold values from 0 to 15, as said below
- plus_flux: float32 [4, 384, 384], P('spec'), may hold values from -0.3125 to 0.3125
- minus_flux: float32 [4, 384, 384], P('spec'), may hold values from -0.3125 to 0.3125
- face_limiter: int32 [4, 1024], P('spec', 'cell'), may hold values from 0 to 2
Outputs:
- new_field: float32 [4, 1024, 384], P('spec', 'cell')
- collision: float32 [4, 1024, 384], P('spec', 'cell')
Inputs may be any that keep to these rules, and one draw needn't show every extreme that they name: Row s of pair_table names each of the tensors s * 4 to s * 4 + 3 exactly once. `face_limiter`: 0 first order, 1 minmod slope, 2 monotonized central slope.
All inputs are finite; a program needn't handle non-finite values.
Results may differ from a plain program's by a relative error of at most 0.0004.
Values may be sent and summed in bfloat16 or wider, within the bound.
A program may use at most 64 MiB of HBM per device.

v0:
```python
import jax
import jax.numpy as jnp
from jax import lax
from jax.sharding import PartitionSpec as P


def with_halo(x, sides, width):
    for axis, dim in sides:
        size, length = (lax.axis_size(axis), x.shape[dim])
        up = [(i, (i + 1) % size) for i in range(size)]
        down = [(j, i) for i, j in up]
        last = lax.slice_in_dim(x, length - width, length, axis=dim)
        leading = lax.slice_in_dim(x, 0, width, axis=dim)
        before = lax.ppermute(last, axis, up)
        after = lax.ppermute(leading, axis, down)
        x = jnp.concatenate([before, x, after], axis=dim)
    return x


def shifted(x, axis, by):
    size = lax.axis_size(axis)
    return lax.ppermute(x, axis, [(i, (i + by) % size) for i in range(size)])


def minmod_two(first, second):
    return jnp.where(
        first * second > 0, jnp.sign(first) * jnp.minimum(jnp.abs(first), jnp.abs(second)), 0.0
    )


def minmod_three(first, second, third):
    same = (first * second > 0) & (second * third > 0)
    least = jnp.minimum(jnp.minimum(jnp.abs(first), jnp.abs(second)), jnp.abs(third))
    return jnp.where(same, jnp.sign(first) * least, 0.0)


def local(fields, tensors, pair_table, plus_flux, minus_flux, face_limiter):
    cells = fields.shape[1]
    species = lax.axis_size("spec")
    owner = lax.axis_index("spec")
    total_cells = cells * lax.axis_size("cell")
    out_modes = tensors.shape[1]
    table_row = lax.dynamic_index_in_dim(pair_table, owner, 0, keepdims=False)
    all_species = lax.all_gather(fields, "spec", axis=0, tiled=True)
    gathered = lax.all_gather(all_species, "cell", axis=1, tiled=True)
    own_rows = lax.dynamic_index_in_dim(gathered, owner, 0, keepdims=True)
    own_wide = own_rows[0].astype(jnp.float32)
    collision_part = jnp.zeros((total_cells, out_modes), jnp.float32)
    for partner in range(species):
        partner_rows = gathered[partner]
        local_pair = table_row[partner] - owner * species
        tensor = lax.dynamic_index_in_dim(tensors, local_pair, 0, keepdims=False)
        inner = jnp.einsum("cj,kij->cki", partner_rows, tensor, preferred_element_type=jnp.float32)
        collision_part = collision_part + jnp.einsum(
            "cki,ci->ck",
            inner,
            own_wide,
            precision=lax.Precision.HIGHEST,
            preferred_element_type=jnp.float32,
        )
    collision = lax.all_to_all(collision_part, "cell", split_axis=0, concat_axis=1, tiled=True)
    extended = with_halo(fields, (("cell", 1),), 2)
    wide = extended[0].astype(jnp.float32)
    prior_flag = shifted(face_limiter[:, -1:], "cell", 1)
    flags = jnp.concatenate([prior_flag, face_limiter], axis=1)[0][:, None]
    lower = wide[1:-1] - wide[:-2]
    upper = wide[2:] - wide[1:-1]
    slope_one = minmod_two(lower, upper)
    slope_two = minmod_three(2.0 * lower, 0.5 * (lower + upper), 2.0 * upper)
    zero = jnp.zeros((cells + 1, wide.shape[1]), jnp.float32)
    here = jnp.where(flags == 1, slope_one[:-1], jnp.where(flags == 2, slope_two[:-1], zero))
    there = jnp.where(flags == 1, slope_one[1:], jnp.where(flags == 2, slope_two[1:], zero))
    left_state = wide[1 : cells + 2] + 0.5 * here
    right_state = wide[2 : cells + 3] - 0.5 * there
    flux = jnp.dot(
        left_state,
        plus_flux[0],
        precision=lax.Precision.HIGHEST,
        preferred_element_type=jnp.float32,
    )
    flux = flux + jnp.dot(
        right_state,
        minus_flux[0],
        precision=lax.Precision.HIGHEST,
        preferred_element_type=jnp.float32,
    )
    center = wide[2 : cells + 2]
    new_field = center + 0.4 * (flux[:-1] - flux[1:]) + 0.5 * collision
    return (new_field[None], collision[None])


def solution(mesh):
    placed = (
        P("spec", "cell", None),
        P("spec", "cell", None, None),
        P(),
        P("spec", None, None),
        P("spec", None, None),
        P("spec", "cell"),
    )
    return jax.shard_map(
        local,
        mesh=mesh,
        in_specs=placed,
        out_specs=(P("spec", "cell", None), P("spec", "cell", None)),
        check_vma=False,
    )
```

profile of v0, /device:TPU:0, one launch (start us, length us, event | category | flops | bytes accessed | tf_op | source)
XLA Modules:
  0.0 144.8 jit_solution(16800425540163569697)
XLA Ops:
  7.2 0.0 copy-start
  7.2 0.0 all-gather.2.cloned.1.call-start
  7.2 7.1 %all_gather.6 = bf16[4,32,384]{2,1,0:T(8,128)(2,1)} all-gather(bf16[1,32,384]{2,1,0:T(8,128)(2,1)} %param.6), channel_id=1, replica_groups=mesh['cell'=32,'spec'=4] {'spec'}, dimensions={0}, use_global_device_ids=true | all-gather | bytes 122880 | tf_op jit(solution)/shard_map/all_gather | solution.py:44
  14.3 0.0 all-gather.2.cloned.1.call-update
  14.4 0.7 fusion.46
  15.1 8.6 %collective-permute-start.1 = (bf16[1,2,384]{2,1,0:T(2,128)(2,1)S(1)}, bf16[1,2,384]{2,1,0:T(2,128)(2,1)S(1)}, u32[]{:S(2)}, u32[]{:S(2)}) collective-permute-start(bf16[1,2,384]{2,1,0:T(2,128)(2,1)S(1)} %get-tuple-element.9), channel_id=1, source_target_pairs={{4,0},{8,4},{12,8},{16,12},{20,16},{24,20},{28,24},{32,28},{36,32}... | collective-permute-start | bytes 4616 | tf_op jit(solution)/shard_map/ppermute | solution.py:15
  23.6 0.0 collective-permute-start
  23.6 1.3 slice.92
  24.9 0.0 collective-permute-start.2
  24.9 0.7 constant_dynamic-slice_fusion
  25.6 0.6 fusion.47
  28.7 5.7 %collective-permute-done.2 = s32[1,1]{1,0:T(1,128)} collective-permute-done((s32[1,1]{1,0:T(1,128)}, s32[1,1]{1,0:T(1,128)}, u32[]{:S(2)}, u32[]{:S(2)}) %collective-permute-start.2) | collective-permute-done | bytes 36 | tf_op jit(solution)/shard_map/ppermute | solution.py:22
  34.4 1.4 compare_bitcast_fusion.1
  35.7 0.0 collective-permute-done.1
  35.7 0.0 collective-permute-done
  35.7 0.8 maximum_convert_fusion
  36.5 0.1 multiply_select_fusion.1
  36.6 0.0 copy-done
  36.6 0.5 fusion.13
  37.1 54.5 %all-gather.2.cloned.1.call-done = bf16[4,1024,384]{2,1,0:T(8,128)(2,1)} async-done(((bf16[4,32,384]{2,1,0:T(8,128)(2,1)}), bf16[4,1024,384]{2,1,0:T(8,128)(2,1)}) %all-gather.2.cloned.1.call-update) | async-done | bytes 3145744 | tf_op jit(solution)/shard_map/all_gather | solution.py:45
  91.5 1.2 bitcast_convert_fusion
  92.8 1.6 %copy.39 = f32[1024,384]{0,1:T(8,128)} copy(f32[1024,384]{1,0:T(8,128)S(1)} %bitcast_convert_fusion) | data formatting | bytes 3145728
  94.4 0.0 copy-start.1
  94.4 0.0 copy-start.3
  94.4 0.0 copy-start.4
  94.4 7.9 %fusion = f32[1024,12]{0,1:T(8,128)S(1)} fusion(f32[1024,384]{0,1:T(8,128)} %copy.39, bf16[4,12,384,384]{3,2,1,0:T(8,128)(2,1)} %param.7, s32[]{:T(128)S(6)} %select_n.49, bf16[4,1024,384]{2,1,0:T(8,128)(2,1)} %all-gather.2.cloned.1.call-done), kind=kOutput, calls=%fused_computation.1 | convolution fusion | flops 3633303552 | bytes 5947396 | tf_op jit(solution)/shard_map/cj,kij->cki/dot_general | solution.py:53
  102.3 0.0 copy-done.1
  102.3 0.0 copy-done.3
  102.3 0.3 copy-done.4
  102.6 5.6 %fusion.1 = f32[1024,12]{0,1:T(8,128)S(1)} fusion(f32[1024,384]{0,1:T(8,128)S(1)} %copy-done.1, bf16[4,12,384,384]{3,2,1,0:T(8,128)(2,1)S(1)} %copy-done.4, s32[]{:T(128)S(6)} %select_n.48, bf16[4,1024,384]{2,1,0:T(8,128)(2,1)S(1)} %copy-done.3), kind=kOutput, calls=%fused_computation.3 | convolution fusion | flops 3633303552 | bytes 5947396 | tf_op jit(solution)/shard_map/cj,kij->cki/dot_general | solution.py:53
  108.2 5.6 %fusion.3 = f32[1024,12]{0,1:T(8,128)S(1)} fusion(f32[1024,384]{0,1:T(8,128)S(1)} %copy-done.1, bf16[4,12,384,384]{3,2,1,0:T(8,128)(2,1)S(1)} %copy-done.4, s32[]{:T(128)S(6)} %select_n.46, bf16[4,1024,384]{2,1,0:T(8,128)(2,1)S(1)} %copy-done.3), kind=kOutput, calls=%fused_computation.7 | convolution fusion | flops 3633303552 | bytes 5947396 | tf_op jit(solution)/shard_map/cj,kij->cki/dot_general | solution.py:53
  113.8 0.0 copy-start.2
  113.9 5.6 %fusion.2 = f32[1024,12]{0,1:T(8,128)S(1)} fusion(f32[1024,384]{0,1:T(8,128)S(1)} %copy-done.1, bf16[4,12,384,384]{3,2,1,0:T(8,128)(2,1)S(1)} %copy-done.4, s32[]{:T(128)S(6)} %select_n.47, bf16[4,1024,384]{2,1,0:T(8,128)(2,1)S(1)} %copy-done.3), kind=kOutput, calls=%fused_computation.5 | convolution fusion | flops 3633303552 | bytes 5947396 | tf_op jit(solution)/shard_map/cj,kij->cki/dot_general | solution.py:53
  119.5 0.1 all_to_all.12
  119.6 0.1 copy.42
  119.8 0.8 reshape.94
  120.5 4.7 %all-to-all-start = ((f32[32,1,384]{2,1,0:T(1,128)}), f32[32,1,384]{2,1,0:T(1,128)S(1)}, u32[]{:S(2)}, u32[]{:S(2)}) async-start(f32[32,1,384]{2,1,0:T(1,128)} %reshape.94), calls=%async_computation | async-start | bytes 98304 | tf_op jit(solution)/shard_map/all_to_all | solution.py:61
  125.2 0.0 copy-done.2
  125.2 0.5 convolution_add_fusion
  125.7 9.3 %all-to-all-done = f32[32,1,384]{2,1,0:T(1,128)S(1)} async-done(((f32[32,1,384]{2,1,0:T(1,128)}), f32[32,1,384]{2,1,0:T(1,128)S(1)}, u32[]{:S(2)}, u32[]{:S(2)}) %all-to-all-start) | async-done | bytes 49184 | tf_op jit(solution)/shard_map/all_to_all | solution.py:61
  135.0 0.5 broadcast.69
  135.5 0.8 reduce.8
  136.3 0.1 reshape.95
  136.5 0.1 copy.13
  136.6 0.7 copy.14
  137.3 0.6 fusion.29
  (5 shorter events, 0.1 us)
Async XLA Ops:
  7.2 29.4 %copy-start = (f32[1,384,384]{2,1,0:T(8,128)S(1)}, f32[1,384,384]{2,1,0:T(8,128)}, u32[]{:S(2)}) copy-start(f32[1,384,384]{2,1,0:T(8,128)} %param.9) | copy-start | bytes 1769476
  7.2 84.3 %all-gather.2.cloned.1.call-start = ((), (), s32[]{:S(2)}) async-start(), calls=%async_computation.1 | async-start | bytes 3244032 | tf_op jit(solution)/shard_map/all_gather | solution.py:45
  15.1 20.7 %collective-permute-start.1 = (bf16[1,2,384]{2,1,0:T(2,128)(2,1)S(1)}, bf16[1,2,384]{2,1,0:T(2,128)(2,1)S(1)}, u32[]{:S(2)}, u32[]{:S(2)}) collective-permute-start(bf16[1,2,384]{2,1,0:T(2,128)(2,1)S(1)} %get-tuple-element.9), channel_id=1, source_target_pairs={{4,0},{8,4},{12,8},{16,12},{20,16},{24,20},{28,24},{32,28},{36,32}... | collective-permute-start | bytes 4616 | tf_op jit(solution)/shard_map/ppermute | solution.py:15
  23.6 12.1 %collective-permute-start = (bf16[1,2,384]{2,1,0:T(2,128)(2,1)S(1)}, bf16[1,2,384]{2,1,0:T(2,128)(2,1)S(1)}, u32[]{:S(2)}, u32[]{:S(2)}) collective-permute-start(bf16[1,2,384]{2,1,0:T(2,128)(2,1)S(1)} %get-tuple-element.8), channel_id=1, source_target_pairs={{0,4},{4,8},{8,12},{12,16},{16,20},{20,24},{24,28},{28,32},{32,36}... | collective-permute-start | bytes 4616 | tf_op jit(solution)/shard_map/ppermute | solution.py:14
  24.9 9.5 %collective-permute-start.2 = (s32[1,1]{1,0:T(1,128)}, s32[1,1]{1,0:T(1,128)}, u32[]{:S(2)}, u32[]{:S(2)}) collective-permute-start(s32[1,1]{1,0:T(1,128)} %slice.92), channel_id=1, source_target_pairs={{0,4},{4,8},{8,12},{12,16},{16,20},{20,24},{24,28},{28,32},{32,36}... | collective-permute-start | bytes 20 | tf_op jit(solution)/shard_map/ppermute | solution.py:22
  94.4 7.9 %copy-start.1 = (f32[1024,384]{0,1:T(8,128)S(1)}, f32[1024,384]{0,1:T(8,128)}, u32[]{:S(2)}) copy-start(f32[1024,384]{0,1:T(8,128)} %copy.39) | copy-start | bytes 4718596
  94.4 7.9 %copy-start.3 = (bf16[4,1024,384]{2,1,0:T(8,128)(2,1)S(1)}, bf16[4,1024,384]{2,1,0:T(8,128)(2,1)}, u32[]{:S(2)}) copy-start(bf16[4,1024,384]{2,1,0:T(8,128)(2,1)} %all-gather.2.cloned.1.call-done) | copy-start | bytes 9437188
  94.4 8.2 %copy-start.4 = (bf16[4,12,384,384]{3,2,1,0:T(8,128)(2,1)S(1)}, bf16[4,12,384,384]{3,2,1,0:T(8,128)(2,1)}, u32[]{:S(2)}) copy-start(bf16[4,12,384,384]{3,2,1,0:T(8,128)(2,1)} %param.7) | copy-start | bytes 42467332
  113.8 11.4 %copy-start.2 = (f32[1,384,384]{2,1,0:T(8,128)S(1)}, f32[1,384,384]{2,1,0:T(8,128)}, u32[]{:S(2)}) copy-start(f32[1,384,384]{2,1,0:T(8,128)} %param.10) | copy-start | bytes 1769476
  120.5 14.5 %all-to-all-start = ((f32[32,1,384]{2,1,0:T(1,128)}), f32[32,1,384]{2,1,0:T(1,128)S(1)}, u32[]{:S(2)}, u32[]{:S(2)}) async-start(f32[32,1,384]{2,1,0:T(1,128)} %reshape.94), calls=%async_computation | async-start | bytes 98304 | tf_op jit(solution)/shard_map/all_to_all | solution.py:61
Sparse Core Ops, SparseCore 0:
  14.5 76.9 all-gather.1
where the time goes:
time: 145 us
  waiting for transfers between devices  69.4 us (48%)
  matrix products  25.7 us (18%)
  between operations  16.7 us (12%)
  starting transfers between devices  13.3 us (9%)
  local copies, waits for them, and re-layouts  7.71 us (5%)
  blocking collectives  7.11 us (5%)
  other arithmetic  4.88 us (3%)
    all_gather x1, waiting for transfers between devices, local(): gathered = lax.all_gather(all_species, 'cell', axis=1, tiled=True)  54.5 us
    dot_general x4, matrix products, local(): jnp.einsum('cj,kij->cki', partner_rows, tensor, preferred_element_type=jn...  24.7 us
    all_to_all x1, waiting for transfers between devices, local(): lax.all_to_all(collision_part, 'cell', split_axis=0, concat_axis=1, tiled...  9.3 us
    ppermute x1, starting transfers between devices, with_halo(): after = lax.ppermute(leading, axis, down)  8.57 us
    all_gather x1, blocking collectives, local(): all_species = lax.all_gather(fields, 'spec', axis=0, tiled=True)  7.11 us
    ppermute x1, waiting for transfers between devices, shifted(): return lax.ppermute(x, axis, [(i, (i + by) % size) for i in range(size)])  5.67 us
    all_to_all x1, starting transfers between devices, local(): lax.all_to_all(collision_part, 'cell', split_axis=0, concat_axis=1, tiled...  4.7 us
    unnamed x14, local copies, waits for them, and re-layouts  3.55 us
  transfers between devices with their start and end apart: 5, of which 3 were waited for; matrix products, arithmetic and copies ran while one was open for 4% of the time, Pallas kernels for 0%

commit v1 on v0

--- a/solution.py
+++ b/solution.py
@@ -42,7 +42,8 @@
     out_modes = tensors.shape[1]
     table_row = lax.dynamic_index_in_dim(pair_table, owner, 0, keepdims=False)
     all_species = lax.all_gather(fields, "spec", axis=0, tiled=True)
-    gathered = lax.all_gather(all_species, "cell", axis=1, tiled=True)
+    outgoing = jnp.stack([all_species] * lax.axis_size("cell"))
+    gathered = jnp.concatenate(lax.all_to_all(outgoing, "cell", 0, 0), axis=1)
     own_rows = lax.dynamic_index_in_dim(gathered, owner, 0, keepdims=True)
     own_wide = own_rows[0].astype(jnp.float32)
     collision_part = jnp.zeros((total_cells, out_modes), jnp.float32)

time: 145 us -> 119 us (0.82)
  waiting for transfers between devices: 69.4 us -> 36.6 us
  starting transfers between devices: 13.3 us -> 26.6 us
  between operations: 16.7 us -> 3.48 us
  local copies, waits for them, and re-layouts: 7.71 us -> 15.9 us
    all_gather x1 -> x0, waiting for transfers between devices: 54.5 us -> none  [local(): gathered = lax.all_gather(all_species, 'cell', axis=1, tiled=True)]
    ppermute x1, waiting for transfers between devices: 5.67 us -> 27.3 us  [shifted(): return lax.ppermute(x, axis, [(i, (i + by) % size) for i in range(size)])]
    all_to_all x0 -> x1, starting transfers between devices: none -> 11 us  [local(): gathered = jnp.concatenate(lax.all_to_all(outgoing, 'cell', 0, 0), axis=1)]
    all_to_all x1, starting transfers between devices: 4.7 us -> 7.95 us  [local(): lax.all_to_all(collision_part, 'cell', split_axis=0, concat_axis=1, tiled...]
    slice x0 -> x1, local copies, waits for them, and re-layouts: none -> 2.33 us  [local(): partner_rows = gathered[partner]]
    all_to_all x0 -> x1, local copies, waits for them, and re-layouts: none -> 2.29 us  [local(): gathered = jnp.concatenate(lax.all_to_all(outgoing, 'cell', 0, 0), axis=1)]
    another operation x0 -> x1, local copies, waits for them, and re-layouts: none -> 2.17 us  [local(): outgoing = jnp.stack([all_species] * lax.axis_size('cell'))]
    unnamed x14 -> x20, local copies, waits for them, and re-layouts: 3.55 us -> 4.89 us
  transfers between devices with their start and end apart: 5 -> 5, of which waited for: 3 -> 2; matrix products, arithmetic and copies ran while one was open for 4% -> 5% of each run, Pallas kernels for 0% -> 0%
where the time goes in v1:
time: 119 us; the launch traced here: 118 us
  waiting for transfers between devices  36.6 us (31%)
  starting transfers between devices  26.6 us (22%)
  matrix products  25.7 us (22%)
  local copies, waits for them, and re-layouts  15.9 us (13%)
  blocking collectives  5.67 us (5%)
  other arithmetic  3.75 us (3%)
  between operations  3.48 us (3%)
    ppermute x1, waiting for transfers between devices, shifted(): return lax.ppermute(x, axis, [(i, (i + by) % size) for i in range(size)])  27.3 us
    dot_general x4, matrix products, local(): jnp.einsum('cj,kij->cki', partner_rows, tensor, preferred_element_type=jn...  24.8 us
    all_to_all x1, starting transfers between devices, local(): gathered = jnp.concatenate(lax.all_to_all(outgoing, 'cell', 0, 0), axis=1)  11 us
    all_to_all x1, waiting for transfers between devices, local(): lax.all_to_all(collision_part, 'cell', split_axis=0, concat_axis=1, tiled...  9.3 us
    all_to_all x1, starting transfers between devices, local(): lax.all_to_all(collision_part, 'cell', split_axis=0, concat_axis=1, tiled...  7.95 us
    ppermute x1, starting transfers between devices, with_halo(): after = lax.ppermute(leading, axis, down)  7.54 us
    all_gather x1, blocking collectives, local(): all_species = lax.all_gather(fields, 'spec', axis=0, tiled=True)  5.67 us
    unnamed x20, local copies, waits for them, and re-layouts  4.89 us
  transfers between devices with their start and end apart: 5, of which 2 were waited for; matrix products, arithmetic and copies ran while one was open for 5% of the time, Pallas kernels for 0%

profile of v1, /device:TPU:0, one launch (start us, length us, event | category | flops | bytes accessed | tf_op | source)
XLA Modules:
  0.0 117.8 jit_solution(5173710136335667267)
XLA Ops:
  0.6 0.0 copy-start
  0.6 5.7 %all_gather.3 = bf16[4,32,384]{2,1,0:T(8,128)(2,1)S(1)} all-gather(bf16[1,32,384]{2,1,0:T(8,128)(2,1)} %param.6), channel_id=1, replica_groups=mesh['cell'=32,'spec'=4] {'spec'}, dimensions={0}, use_global_device_ids=true | all-gather | bytes 122880 | tf_op jit(solution)/shard_map/all_gather | solution.py:44
  6.3 2.2 %stack.2 = bf16[32,4,32,384]{3,2,1,0:T(8,128)(2,1)} broadcast(bf16[4,32,384]{2,1,0:T(8,128)(2,1)S(1)} %all_gather.3), dimensions={1,2,3} | broadcast | bytes 3244032 | tf_op jit(solution)/shard_map/stack | solution.py:45
  8.5 11.0 %all-to-all-start = ((bf16[32,4,32,384]{3,2,1,0:T(8,128)(2,1)}), bf16[32,4,32,384]{3,2,1,0:T(8,128)(2,1)}, u32[]{:S(2)}, u32[]{:S(2)}) async-start(bf16[32,4,32,384]{3,2,1,0:T(8,128)(2,1)} %stack.2), calls=%async_computation | async-start | bytes 6291456 | tf_op jit(solution)/shard_map/all_to_all | solution.py:46
  19.5 0.7 fusion.47
  20.2 7.5 %collective-permute-start.1 = (bf16[1,2,384]{2,1,0:T(2,128)(2,1)S(1)}, bf16[1,2,384]{2,1,0:T(2,128)(2,1)S(1)}, u32[]{:S(2)}, u32[]{:S(2)}) collective-permute-start(bf16[1,2,384]{2,1,0:T(2,128)(2,1)S(1)} %get-tuple-element.15), channel_id=1, source_target_pairs={{4,0},{8,4},{12,8},{16,12},{20,16},{24,20},{28,24},{32,28},{36,32}... | collective-permute-start | bytes 4616 | tf_op jit(solution)/shard_map/ppermute | solution.py:15
  27.8 0.0 collective-permute-start
  27.8 1.3 %slice.96 = s32[1,1]{1,0:T(1,128)} slice(s32[1,32]{1,0:T(1,128)} %param.11), slice={[0:1], [31:32]} | slice | bytes 8 | tf_op jit(solution)/shard_map/slice | solution.py:65
  29.0 0.1 collective-permute-start.2
  29.1 0.7 constant_dynamic-slice_fusion
  29.8 0.7 fusion.48
  33.1 27.3 %collective-permute-done.2 = s32[1,1]{1,0:T(1,128)} collective-permute-done((s32[1,1]{1,0:T(1,128)}, s32[1,1]{1,0:T(1,128)}, u32[]{:S(2)}, u32[]{:S(2)}) %collective-permute-start.2) | collective-permute-done | bytes 36 | tf_op jit(solution)/shard_map/ppermute | solution.py:22
  60.4 1.4 %compare_bitcast_fusion.1 = (pred[33]{0:T(512)(128)(4,1)S(1)}, pred[33]{0:T(512)(128)(4,1)S(1)}) fusion(s32[1,32]{1,0:T(1,128)} %param.11, s32[1,1]{1,0:T(1,128)} %collective-permute-done.2), kind=kLoop, calls=%fused_computation.62 | loop fusion | flops 99 | bytes 198 | tf_op jit(solution)/shard_map/eq | solution.py:72
  61.8 0.0 collective-permute-done.1
  61.8 0.0 collective-permute-done
  61.8 0.8 maximum_convert_fusion
  62.5 0.1 multiply_select_fusion.1
  62.6 0.0 copy-done
  62.7 0.5 fusion.13
  63.1 0.0 all-to-all-done
  63.1 2.3 %copy.45 = bf16[32,4,32,384]{3,2,0,1:T(8,128)(2,1)S(1)} copy(bf16[32,4,32,384]{3,2,1,0:T(8,128)(2,1)} %all-to-all-done) | data formatting | bytes 6291456 | tf_op jit(solution)/shard_map/all_to_all | solution.py:46
  65.4 0.0 copy-start.1
  65.4 1.6 %copy-done.1 = bf16[32,4,32,384]{3,2,0,1:T(8,128)(2,1)} copy-done((bf16[32,4,32,384]{3,2,0,1:T(8,128)(2,1)}, bf16[32,4,32,384]{3,2,0,1:T(8,128)(2,1)S(1)}, u32[]{:S(2)}) %copy-start.1) | copy-done | bytes 3145752
  67.1 0.1 bitcast_convert_fusion
  67.2 1.6 %copy.40 = f32[1024,384]{0,1:T(8,128)} copy(f32[1024,384]{1,0:T(8,128)S(1)} %bitcast_convert_fusion) | data formatting | bytes 3145728
  68.8 2.3 %fusion.46 = (bf16[1,32,32,384]{3,2,1,0:T(8,128)(2,1)S(1)}, bf16[1,32,32,384]{3,2,1,0:T(8,128)(2,1)S(1)}, bf16[1,32,32,384]{3,2,1,0:T(8,128)(2,1)S(1)}, bf16[1,32,32,384]{3,2,1,0:T(8,128)(2,1)S(1)}) fusion(bf16[4,32,32,384]{3,2,1,0:T(8,128)(2,1)} %bitcast.137), kind=kLoop, calls=%fused_computation.74 | loop fusion | bytes 6291456 | tf_op jit(solution)/shard_map/slice | solution.py:51
  71.1 0.0 slice-start.1
  71.1 0.0 slice-start.2
  71.2 0.0 slice-start.3
  71.2 7.9 %fusion = f32[1024,12]{0,1:T(8,128)S(1)} fusion(f32[1024,384]{0,1:T(8,128)} %copy.40, bf16[1024,384,1]{1,0,2:T(8,128)(2,1)S(1)} %bitcast.142, bf16[4,12,384,384]{3,2,1,0:T(8,128)(2,1)} %param.7, s32[]{:T(128)S(6)} %select_n.49), kind=kOutput, calls=%fused_computation.1 | convolution fusion | flops 3633303552 | bytes 5947396 | tf_op jit(solution)/shard_map/cj,kij->cki/dot_general | solution.py:54
  79.1 0.0 copy-done.2
  79.1 0.0 slice-done
  79.2 5.6 %fusion.1 = f32[1024,12]{0,1:T(8,128)S(1)} fusion(f32[1024,384]{0,1:T(8,128)S(1)} %copy-done.2, bf16[1024,384,1]{1,0,2:T(8,128)(2,1)S(1)} %bitcast.141, bf16[4,12,384,384]{3,2,1,0:T(8,128)(2,1)S(1)} %bitcast.144, s32[]{:T(128)S(6)} %select_n.48), kind=kOutput, calls=%fused_computation.3 | convolution fusion | flops 3633303552 | bytes 5947396 | tf_op jit(solution)/shard_map/cj,kij->cki/dot_general | solution.py:54
  84.8 5.6 %fusion.3 = f32[1024,12]{0,1:T(8,128)S(1)} fusion(f32[1024,384]{0,1:T(8,128)S(1)} %copy-done.2, bf16[1024,384,1]{1,0,2:T(8,128)(2,1)S(1)} %bitcast.140, bf16[4,12,384,384]{3,2,1,0:T(8,128)(2,1)S(1)} %bitcast.144, s32[]{:T(128)S(6)} %select_n.46), kind=kOutput, calls=%fused_computation.7 | convolution fusion | flops 3633303552 | bytes 5947396 | tf_op jit(solution)/shard_map/cj,kij->cki/dot_general | solution.py:54
  90.4 0.0 copy-start.3
  90.4 5.6 %fusion.2 = f32[1024,12]{0,1:T(8,128)S(1)} fusion(f32[1024,384]{0,1:T(8,128)S(1)} %copy-done.2, bf16[1024,384,1]{1,0,2:T(8,128)(2,1)S(1)} %bitcast.139, bf16[4,12,384,384]{3,2,1,0:T(8,128)(2,1)S(1)} %bitcast.144, s32[]{:T(128)S(6)} %select_n.47), kind=kOutput, calls=%fused_computation.5 | convolution fusion | flops 3633303552 | bytes 5947396 | tf_op jit(solution)/shard_map/cj,kij->cki/dot_general | solution.py:54
  96.1 0.1 all_to_all.16
  96.2 0.1 copy.46
  96.3 0.8 reshape.112
  97.1 7.9 %all-to-all-start.1 = ((f32[32,1,384]{2,1,0:T(1,128)}), f32[32,1,384]{2,1,0:T(1,128)S(1)}, u32[]{:S(2)}, u32[]{:S(2)}) async-start(f32[32,1,384]{2,1,0:T(1,128)} %reshape.112), calls=%async_computation.1 | async-start | bytes 98304 | tf_op jit(solution)/shard_map/all_to_all | solution.py:62
  105.1 0.5 convolution_add_fusion
  105.5 9.3 %all-to-all-done.1 = f32[32,1,384]{2,1,0:T(1,128)S(1)} async-done(((f32[32,1,384]{2,1,0:T(1,128)}), f32[32,1,384]{2,1,0:T(1,128)S(1)}, u32[]{:S(2)}, u32[]{:S(2)}) %all-to-all-start.1) | async-done | bytes 49184 | tf_op jit(solution)/shard_map/all_to_all | solution.py:62
  114.8 0.5 broadcast.71
  115.3 0.8 reduce.8
  116.1 0.1 reshape.113
  116.3 0.1 copy.14
  116.4 0.7 copy.15
  117.2 0.6 fusion.29
  (12 shorter events, 0.1 us)
Async XLA Ops:
  0.6 62.0 %copy-start = (f32[1,384,384]{2,1,0:T(8,128)S(1)}, f32[1,384,384]{2,1,0:T(8,128)}, u32[]{:S(2)}) copy-start(f32[1,384,384]{2,1,0:T(8,128)} %param.9) | copy-start | bytes 1769476
  8.5 54.6 %all-to-all-start = ((bf16[32,4,32,384]{3,2,1,0:T(8,128)(2,1)}), bf16[32,4,32,384]{3,2,1,0:T(8,128)(2,1)}, u32[]{:S(2)}, u32[]{:S(2)}) async-start(bf16[32,4,32,384]{3,2,1,0:T(8,128)(2,1)} %stack.2), calls=%async_computation | async-start | bytes 6291456 | tf_op jit(solution)/shard_map/all_to_all | solution.py:46
  20.2 41.6 %collective-permute-start.1 = (bf16[1,2,384]{2,1,0:T(2,128)(2,1)S(1)}, bf16[1,2,384]{2,1,0:T(2,128)(2,1)S(1)}, u32[]{:S(2)}, u32[]{:S(2)}) collective-permute-start(bf16[1,2,384]{2,1,0:T(2,128)(2,1)S(1)} %get-tuple-element.15), channel_id=1, source_target_pairs={{4,0},{8,4},{12,8},{16,12},{20,16},{24,20},{28,24},{32,28},{36,32}... | collective-permute-start | bytes 4616 | tf_op jit(solution)/shard_map/ppermute | solution.py:15
  27.8 34.0 %collective-permute-start = (bf16[1,2,384]{2,1,0:T(2,128)(2,1)S(1)}, bf16[1,2,384]{2,1,0:T(2,128)(2,1)S(1)}, u32[]{:S(2)}, u32[]{:S(2)}) collective-permute-start(bf16[1,2,384]{2,1,0:T(2,128)(2,1)S(1)} %get-tuple-element.14), channel_id=1, source_target_pairs={{0,4},{4,8},{8,12},{12,16},{16,20},{20,24},{24,28},{28,32},{32,36}... | collective-permute-start | bytes 4616 | tf_op jit(solution)/shard_map/ppermute | solution.py:14
  29.0 31.4 %collective-permute-start.2 = (s32[1,1]{1,0:T(1,128)}, s32[1,1]{1,0:T(1,128)}, u32[]{:S(2)}, u32[]{:S(2)}) collective-permute-start(s32[1,1]{1,0:T(1,128)} %slice.96), channel_id=1, source_target_pairs={{0,4},{4,8},{8,12},{12,16},{16,20},{20,24},{24,28},{28,32},{32,36}... | collective-permute-start | bytes 20 | tf_op jit(solution)/shard_map/ppermute | solution.py:22
  65.4 1.6 %copy-start.1 = (bf16[32,4,32,384]{3,2,0,1:T(8,128)(2,1)}, bf16[32,4,32,384]{3,2,0,1:T(8,128)(2,1)S(1)}, u32[]{:S(2)}) copy-start(bf16[32,4,32,384]{3,2,0,1:T(8,128)(2,1)S(1)} %copy.45) | copy-start | bytes 9437188
  68.8 10.3 %copy-start.2 = (f32[1024,384]{0,1:T(8,128)S(1)}, f32[1024,384]{0,1:T(8,128)}, u32[]{:S(2)}) copy-start(f32[1024,384]{0,1:T(8,128)} %copy.40) | copy-start | bytes 4718596
  68.8 10.3 %slice-start = ((s8[14155776]{0:T(1024)(128)(4,1)}), s8[4194304]{0:T(1024)(128)(4,1)S(1)}, s32[]{:S(2)}) async-start(s8[14155776]{0:T(1024)(128)(4,1)} %bitcast.143), calls=%async_computation.2 | async-start | bytes 8388608
  71.1 8.0 %slice-start.1 = ((s8[14155776]{0:T(1024)(128)(4,1)}), s8[4194304]{0:T(1024)(128)(4,1)S(1)}, s32[]{:S(2)}) async-start(s8[14155776]{0:T(1024)(128)(4,1)} %bitcast.143), calls=%async_computation.3 | async-start | bytes 8388608
  71.1 8.0 %slice-start.2 = ((s8[14155776]{0:T(1024)(128)(4,1)}), s8[4194304]{0:T(1024)(128)(4,1)S(1)}, s32[]{:S(2)}) async-start(s8[14155776]{0:T(1024)(128)(4,1)} %bitcast.143), calls=%async_computation.4 | async-start | bytes 8388608
  71.2 8.0 %slice-start.3 = ((s8[14155776]{0:T(1024)(128)(4,1)}), s8[1572864]{0:T(1024)(128)(4,1)S(1)}, s32[]{:S(2)}) async-start(s8[14155776]{0:T(1024)(128)(4,1)} %bitcast.143), calls=%async_computation.5 | async-start | bytes 3145728
  90.4 14.6 %copy-start.3 = (f32[1,384,384]{2,1,0:T(8,128)S(1)}, f32[1,384,384]{2,1,0:T(8,128)}, u32[]{:S(2)}) copy-start(f32[1,384,384]{2,1,0:T(8,128)} %param.10) | copy-start | bytes 1769476
  97.1 17.7 %all-to-all-start.1 = ((f32[32,1,384]{2,1,0:T(1,128)}), f32[32,1,384]{2,1,0:T(1,128)S(1)}, u32[]{:S(2)}, u32[]{:S(2)}) async-start(f32[32,1,384]{2,1,0:T(1,128)} %reshape.112), calls=%async_computation.1 | async-start | bytes 98304 | tf_op jit(solution)/shard_map/all_to_all | solution.py:62
